TPU v7x, 256 devices: a whole 4x4x8 slice. The times are simulated.
256 devices in a mesh: dom: 8 (over x, core), st: 32 (over y, z).
Axes of the slice: x: 4, y: 4, z: 8, core: 2. Of those that a mesh axis runs over, the one named last changes fastest.
Arguments:
- orbitals: bfloat16 [512, 512, 1024], P('st', 'dom'), may hold values from -6 to 6
- potential: bfloat16 [512, 1024], P('dom'), may hold values from -0.5 to 0.5
- rotation: bfloat16 [512, 512], P('st'), may hold values from -0.25 to 0.25
Outputs:
- rotated: bfloat16 [512, 524288], P(None, ('dom', 'st'))
All inputs are finite; a program needn't handle non-finite values.
Results may differ from a plain program's by a relative error of at most 0.0049.
Values may be sent and summed in bfloat16 or wider, within the bound.
No kernel may reach another device: no remote copies, remote signals or barrier semaphores. Data moves between devices by JAX's collectives and lax.ppermute only.
A program may use at most 64 MiB of HBM per device.

v0:
```python
import jax
import jax.numpy as jnp
from jax import lax
from jax.sharding import PartitionSpec as P

DEGREE = 4
NZ = 32
cheb_shift = 3.75
cheb_scale = 3.25


def extended(block, sides, width):
    for axis, dim in sides:
        count = lax.axis_size(axis)
        forward = [(i, i + 1) for i in range(count - 1)]
        backward = [(target, source) for source, target in forward]
        low = lax.ppermute(
            lax.slice_in_dim(block, block.shape[dim] - width, None, axis=dim), axis, forward
        )
        high = lax.ppermute(lax.slice_in_dim(block, 0, width, axis=dim), axis, backward)
        block = jnp.concatenate([low, block, high], axis=dim)
    return block


def neighbour_sum(center, nz_count):
    row_width = center.shape[2]
    z_position = lax.broadcasted_iota(jnp.int32, (1, 1, row_width), 2) % nz_count
    padded = jnp.pad(center, ((0, 0), (0, 0), (nz_count, nz_count)))
    along_y = padded[:, :, 2 * nz_count :] + padded[:, :, :row_width]
    upper_z = jnp.where(
        z_position < nz_count - 1, padded[:, :, nz_count + 1 : nz_count + 1 + row_width], 0.0
    )
    lower_z = jnp.where(z_position > 0, padded[:, :, nz_count - 1 : nz_count - 1 + row_width], 0.0)
    return along_y + upper_z + lower_z


def hamiltonian(padded_x, local_pot, nz_count):
    center = padded_x[:, 1:-1]
    beside = padded_x[:, 2:] + padded_x[:, :-2] + neighbour_sum(center, nz_count)
    return (3.0 + local_pot) * center - 0.5 * beside


def chebyshev(start, apply_fn, degree):
    previous = start
    current = (apply_fn(start) - cheb_shift * start) / cheb_scale
    for filter_order in range(1, degree):
        following = 2.0 * (apply_fn(current) - cheb_shift * current) / cheb_scale - previous
        previous = current
        current = following
    return current


def local(orbitals, potential, rotation):
    start = orbitals.astype(jnp.float32)
    local_pot = potential.astype(jnp.float32)
    states_dev, planes, row_width = start.shape

    def apply_step(state_field):
        padded = extended(state_field, (("dom", 1),), 1)
        return hamiltonian(padded, local_pot, NZ)

    result = chebyshev(start, apply_step, DEGREE)
    filtered = result.astype(jnp.bfloat16).reshape(states_dev, planes * row_width)
    regrouped = lax.all_to_all(filtered, "st", split_axis=1, concat_axis=0, tiled=True)
    product = jnp.dot(
        lax.all_gather(rotation, "st", axis=0, tiled=True),
        regrouped,
        preferred_element_type=jnp.float32,
    )
    return product.astype(jnp.bfloat16)


def solution(mesh):
    return jax.shard_map(
        local,
        mesh=mesh,
        in_specs=(P("st", "dom", None), P("dom", None), P("st", None)),
        out_specs=P(None, ("dom", "st")),
        check_vma=False,
    )
```

profile of v0, /device:TPU:2, one launch (start us, length us, event | category | flops | bytes accessed | tf_op | source)
XLA Modules:
  0.0 166.8 jit_solution(14921552852424381821)
XLA Ops:
  0.0 1.1 fusion.57
  1.2 1.9 %collective-permute-start = (f32[16,1,1024]{2,1,0:T(1,128)S(1)}, f32[16,1,1024]{2,1,0:T(1,128)S(1)}, u32[]{:S(2)}, u32[]{:S(2)}) collective-permute-start(f32[16,1,1024]{2,1,0:T(1,128)S(1)} %get-tuple-element.13), channel_id=1, source_target_pairs={{32,0},{64,32},{96,64},{128,96},{160,128},{192,160},{224,192},{33,... | collective-permute-start | bytes 196616 | tf_op jit(solution)/shard_map/ppermute | solution.py:20
  3.1 2.4 %collective-permute-start.1 = (f32[16,1,1024]{2,1,0:T(1,128)S(1)}, f32[16,1,1024]{2,1,0:T(1,128)S(1)}, u32[]{:S(2)}, u32[]{:S(2)}) collective-permute-start(f32[16,1,1024]{2,1,0:T(1,128)S(1)} %get-tuple-element.14), channel_id=1, source_target_pairs={{0,32},{32,64},{64,96},{96,128},{128,160},{160,192},{192,224},{1,3... | collective-permute-start | bytes 196616 | tf_op jit(solution)/shard_map/ppermute | solution.py:17
  5.5 2.0 %convert_element_type.21 = f32[16,64,1024]{2,1,0:T(8,128)S(1)} convert(bf16[16,64,1024]{2,1,0:T(8,128)(2,1)} %param.3) | non-fusion elementwise | flops 1048576 | bytes 6291456 | tf_op jit(solution)/shard_map/convert_element_type | solution.py:54
  7.6 1.6 collective-permute-done.1
  9.3 4.7 %broadcast_multiply_fusion = (f32[16,64,1024]{2,1,0:T(8,128)S(1)}, f32[16,64,1024]{2,1,0:T(8,128)S(1)}) fusion(f32[16,64,1024]{2,1,0:T(8,128)S(1)} %convert_element_type.21, pred[1024]{0:T(1024)(128)(4,1)S(1)} %get-tuple-element.17, pred[1024]{0:T(1024)(128)(4,1)S(1)} %get-tuple-element.18, f32[16,1,1024]{2,1,0:T(1,128)S(1)} %collective-permute-done.1, ...), kind=kLoop, calls=%fused_computation.73 | loop fusion | flops 15728640 | bytes 12978176 | tf_op jit(solution)/shard_map/div | solution.py:45
  14.0 2.2 %collective-permute-start.2 = (f32[16,1,1024]{2,1,0:T(1,128)S(1)}, f32[16,1,1024]{2,1,0:T(1,128)S(1)}, u32[]{:S(2)}, u32[]{:S(2)}) collective-permute-start(f32[16,1,1024]{2,1,0:T(1,128)S(1)} %get-tuple-element.11), channel_id=1, source_target_pairs={{32,0},{64,32},{96,64},{128,96},{160,128},{192,160},{224,192},{33,... | collective-permute-start | bytes 196616 | tf_op jit(solution)/shard_map/ppermute | solution.py:20
  16.2 2.2 %collective-permute-start.3 = (f32[16,1,1024]{2,1,0:T(1,128)S(1)}, f32[16,1,1024]{2,1,0:T(1,128)S(1)}, u32[]{:S(2)}, u32[]{:S(2)}) collective-permute-start(f32[16,1,1024]{2,1,0:T(1,128)S(1)} %get-tuple-element.12), channel_id=1, source_target_pairs={{0,32},{32,64},{64,96},{96,128},{128,160},{160,192},{192,224},{1,3... | collective-permute-start | bytes 196616 | tf_op jit(solution)/shard_map/ppermute | solution.py:17
  18.4 3.4 %collective-permute-done.3 = f32[16,1,1024]{2,1,0:T(1,128)S(1)} collective-permute-done((f32[16,1,1024]{2,1,0:T(1,128)S(1)}, f32[16,1,1024]{2,1,0:T(1,128)S(1)}, u32[]{:S(2)}, u32[]{:S(2)}) %collective-permute-start.3) | collective-permute-done | bytes 65568 | tf_op jit(solution)/shard_map/ppermute | solution.py:17
  21.8 6.1 %fusion.17 = f32[16,64,1024]{2,1,0:T(8,128)S(1)} fusion(f32[16,64,1024]{2,1,0:T(8,128)S(1)} %get-tuple-element.5, f32[16,1,1024]{2,1,0:T(1,128)S(1)} %collective-permute-done.3, f32[16,1,1024]{2,1,0:T(1,128)S(1)} %collective-permute-done.2, f32[16,64,1024]{2,1,0:T(8,128)S(1)} %get-tuple-element.6, f32[64,1024]{1,0:T(8,128)S(1)} %get-tuple-element.15, ...), kind=kLoop, calls=%fused_computation.33 | loop fusion | flops 17825792 | bytes 15075328 | tf_op jit(solution)/shard_map/sub | solution.py:47
  28.0 1.9 %collective-permute-start.4 = (f32[16,1,1024]{2,1,0:T(1,128)S(1)}, f32[16,1,1024]{2,1,0:T(1,128)S(1)}, u32[]{:S(2)}, u32[]{:S(2)}) collective-permute-start(f32[16,1,1024]{2,1,0:T(1,128)S(1)} %get-tuple-element.9), channel_id=1, source_target_pairs={{32,0},{64,32},{96,64},{128,96},{160,128},{192,160},{224,192},{33,... | collective-permute-start | bytes 196616 | tf_op jit(solution)/shard_map/ppermute | solution.py:20
  30.0 2.4 %collective-permute-start.5 = (f32[16,1,1024]{2,1,0:T(1,128)S(1)}, f32[16,1,1024]{2,1,0:T(1,128)S(1)}, u32[]{:S(2)}, u32[]{:S(2)}) collective-permute-start(f32[16,1,1024]{2,1,0:T(1,128)S(1)} %get-tuple-element.10), channel_id=1, source_target_pairs={{0,32},{32,64},{64,96},{96,128},{128,160},{160,192},{192,224},{1,3... | collective-permute-start | bytes 196616 | tf_op jit(solution)/shard_map/ppermute | solution.py:17
  32.4 3.2 %collective-permute-done.5 = f32[16,1,1024]{2,1,0:T(1,128)S(1)} collective-permute-done((f32[16,1,1024]{2,1,0:T(1,128)S(1)}, f32[16,1,1024]{2,1,0:T(1,128)S(1)}, u32[]{:S(2)}, u32[]{:S(2)}) %collective-permute-start.5) | collective-permute-done | bytes 65568 | tf_op jit(solution)/shard_map/ppermute | solution.py:17
  35.6 4.7 %fusion.28 = f32[16,64,1024]{2,1,0:T(8,128)S(1)} fusion(f32[16,64,1024]{2,1,0:T(8,128)S(1)} %fusion.17, f32[16,1,1024]{2,1,0:T(1,128)S(1)} %collective-permute-done.5, f32[16,1,1024]{2,1,0:T(1,128)S(1)} %collective-permute-done.4, f32[16,64,1024]{2,1,0:T(8,128)S(1)} %get-tuple-element.6, f32[64,1024]{1,0:T(8,128)S(1)} %get-tuple-element.16, ...), kind=kLoop, calls=%fused_computation.44 | loop fusion | flops 17825792 | bytes 12978176 | tf_op jit(solution)/shard_map/sub | solution.py:47
  40.4 1.9 %collective-permute-start.6 = (f32[16,1,1024]{2,1,0:T(1,128)S(1)}, f32[16,1,1024]{2,1,0:T(1,128)S(1)}, u32[]{:S(2)}, u32[]{:S(2)}) collective-permute-start(f32[16,1,1024]{2,1,0:T(1,128)S(1)} %get-tuple-element.7), channel_id=1, source_target_pairs={{32,0},{64,32},{96,64},{128,96},{160,128},{192,160},{224,192},{33,... | collective-permute-start | bytes 196616 | tf_op jit(solution)/shard_map/ppermute | solution.py:20
  42.3 2.6 %collective-permute-start.7 = (f32[16,1,1024]{2,1,0:T(1,128)S(1)}, f32[16,1,1024]{2,1,0:T(1,128)S(1)}, u32[]{:S(2)}, u32[]{:S(2)}) collective-permute-start(f32[16,1,1024]{2,1,0:T(1,128)S(1)} %get-tuple-element.8), channel_id=1, source_target_pairs={{0,32},{32,64},{64,96},{96,128},{128,160},{160,192},{192,224},{1,3... | collective-permute-start | bytes 196616 | tf_op jit(solution)/shard_map/ppermute | solution.py:17
  44.9 3.0 %collective-permute-done.7 = f32[16,1,1024]{2,1,0:T(1,128)S(1)} collective-permute-done((f32[16,1,1024]{2,1,0:T(1,128)S(1)}, f32[16,1,1024]{2,1,0:T(1,128)S(1)}, u32[]{:S(2)}, u32[]{:S(2)}) %collective-permute-start.7) | collective-permute-done | bytes 65568 | tf_op jit(solution)/shard_map/ppermute | solution.py:17
  47.9 5.8 %fusion.40 = bf16[16,64,1024]{2,1,0:T(8,128)(2,1)} fusion(f32[16,64,1024]{2,1,0:T(8,128)S(1)} %fusion.17, f32[16,64,1024]{2,1,0:T(8,128)S(1)} %fusion.28, f32[16,1,1024]{2,1,0:T(1,128)S(1)} %collective-permute-done.7, f32[16,1,1024]{2,1,0:T(1,128)S(1)} %collective-permute-done.6, f32[64,1024]{1,0:T(8,128)S(1)} %get-tuple-element.16, ...), kind=kLoop, calls=%fused_computation.56 | loop fusion | flops 17825792 | bytes 10881024 | tf_op jit(solution)/shard_map/convert_element_type | solution.py:63
  53.7 2.7 %all_to_all.14 = bf16[16,32,2048]{2,1,0:T(8,128)(2,1)S(1)} reshape(bf16[16,64,1024]{2,1,0:T(8,128)(2,1)} %fusion.40) | data formatting | bytes 4194304 | tf_op jit(solution)/shard_map/all_to_all | solution.py:64
  56.4 2.5 %copy.8 = bf16[16,32,2048]{2,0,1:T(8,128)(2,1)} copy(bf16[16,32,2048]{2,1,0:T(8,128)(2,1)S(1)} %all_to_all.14) | data formatting | bytes 4194304 | tf_op jit(solution)/shard_map/all_to_all | solution.py:64
  58.8 10.9 %all-to-all-start = ((bf16[16,32,2048]{2,0,1:T(8,128)(2,1)}), bf16[16,32,2048]{2,0,1:T(8,128)(2,1)S(1)}, u32[]{:S(2)}, u32[]{:S(2)}) async-start(bf16[16,32,2048]{2,0,1:T(8,128)(2,1)} %copy.8), calls=%async_computation | async-start | bytes 4194304 | tf_op jit(solution)/shard_map/all_to_all | solution.py:64
  69.7 90.6 %all_gather.3 = bf16[512,512]{1,0:T(8,128)(2,1)S(1)} all-gather(bf16[16,512]{1,0:T(8,128)(2,1)S(1)} %copy-done.1), channel_id=1, replica_groups=mesh['dom'=8,'st'=32] {'st'}, dimensions={0}, use_global_device_ids=true | all-gather | bytes 540672 | tf_op jit(solution)/shard_map/all_gather | solution.py:66
  160.3 2.7 %fusion.47 = bf16[512,2048]{0,1:T(8,128)(2,1)} fusion(bf16[512,2048]{1,0:T(8,128)(2,1)S(1)} %bitcast.7, bf16[512,512]{1,0:T(8,128)(2,1)S(1)} %all_gather.3), kind=kOutput, calls=%fused_computation.72 | convolution fusion | flops 1074790400 | bytes 4718592 | tf_op jit(solution)/shard_map/dot_general | solution.py:65
  162.9 3.9 %copy.9 = bf16[512,2048]{1,0:T(8,128)(2,1)} copy(bf16[512,2048]{0,1:T(8,128)(2,1)} %fusion.47) | data formatting | bytes 4194304 | tf_op jit(solution)/shard_map/convert_element_type | solution.py:70
  (14 shorter events, 0.4 us)
Async XLA Ops:
  0.0 7.6 %copy-start = (bf16[64,1024]{1,0:T(8,128)(2,1)S(1)}, bf16[64,1024]{1,0:T(8,128)(2,1)}, u32[]{:S(2)}) copy-start(bf16[64,1024]{1,0:T(8,128)(2,1)} %param.4) | copy-start | bytes 393220
  1.2 6.5 %collective-permute-start = (f32[16,1,1024]{2,1,0:T(1,128)S(1)}, f32[16,1,1024]{2,1,0:T(1,128)S(1)}, u32[]{:S(2)}, u32[]{:S(2)}) collective-permute-start(f32[16,1,1024]{2,1,0:T(1,128)S(1)} %get-tuple-element.13), channel_id=1, source_target_pairs={{32,0},{64,32},{96,64},{128,96},{160,128},{192,160},{224,192},{33,... | collective-permute-start | bytes 196616 | tf_op jit(solution)/shard_map/ppermute | solution.py:20
  3.1 6.2 %collective-permute-start.1 = (f32[16,1,1024]{2,1,0:T(1,128)S(1)}, f32[16,1,1024]{2,1,0:T(1,128)S(1)}, u32[]{:S(2)}, u32[]{:S(2)}) collective-permute-start(f32[16,1,1024]{2,1,0:T(1,128)S(1)} %get-tuple-element.14), channel_id=1, source_target_pairs={{0,32},{32,64},{64,96},{96,128},{128,160},{160,192},{192,224},{1,3... | collective-permute-start | bytes 196616 | tf_op jit(solution)/shard_map/ppermute | solution.py:17
  14.0 4.3 %collective-permute-start.2 = (f32[16,1,1024]{2,1,0:T(1,128)S(1)}, f32[16,1,1024]{2,1,0:T(1,128)S(1)}, u32[]{:S(2)}, u32[]{:S(2)}) collective-permute-start(f32[16,1,1024]{2,1,0:T(1,128)S(1)} %get-tuple-element.11), channel_id=1, source_target_pairs={{32,0},{64,32},{96,64},{128,96},{160,128},{192,160},{224,192},{33,... | collective-permute-start | bytes 196616 | tf_op jit(solution)/shard_map/ppermute | solution.py:20
  16.2 5.6 %collective-permute-start.3 = (f32[16,1,1024]{2,1,0:T(1,128)S(1)}, f32[16,1,1024]{2,1,0:T(1,128)S(1)}, u32[]{:S(2)}, u32[]{:S(2)}) collective-permute-start(f32[16,1,1024]{2,1,0:T(1,128)S(1)} %get-tuple-element.12), channel_id=1, source_target_pairs={{0,32},{32,64},{64,96},{96,128},{128,160},{160,192},{192,224},{1,3... | collective-permute-start | bytes 196616 | tf_op jit(solution)/shard_map/ppermute | solution.py:17
  28.0 4.3 %collective-permute-start.4 = (f32[16,1,1024]{2,1,0:T(1,128)S(1)}, f32[16,1,1024]{2,1,0:T(1,128)S(1)}, u32[]{:S(2)}, u32[]{:S(2)}) collective-permute-start(f32[16,1,1024]{2,1,0:T(1,128)S(1)} %get-tuple-element.9), channel_id=1, source_target_pairs={{32,0},{64,32},{96,64},{128,96},{160,128},{192,160},{224,192},{33,... | collective-permute-start | bytes 196616 | tf_op jit(solution)/shard_map/ppermute | solution.py:20
  30.0 5.6 %collective-permute-start.5 = (f32[16,1,1024]{2,1,0:T(1,128)S(1)}, f32[16,1,1024]{2,1,0:T(1,128)S(1)}, u32[]{:S(2)}, u32[]{:S(2)}) collective-permute-start(f32[16,1,1024]{2,1,0:T(1,128)S(1)} %get-tuple-element.10), channel_id=1, source_target_pairs={{0,32},{32,64},{64,96},{96,128},{128,160},{160,192},{192,224},{1,3... | collective-permute-start | bytes 196616 | tf_op jit(solution)/shard_map/ppermute | solution.py:17
  40.4 4.5 %collective-permute-start.6 = (f32[16,1,1024]{2,1,0:T(1,128)S(1)}, f32[16,1,1024]{2,1,0:T(1,128)S(1)}, u32[]{:S(2)}, u32[]{:S(2)}) collective-permute-start(f32[16,1,1024]{2,1,0:T(1,128)S(1)} %get-tuple-element.7), channel_id=1, source_target_pairs={{32,0},{64,32},{96,64},{128,96},{160,128},{192,160},{224,192},{33,... | collective-permute-start | bytes 196616 | tf_op jit(solution)/shard_map/ppermute | solution.py:20
  42.3 5.6 %collective-permute-start.7 = (f32[16,1,1024]{2,1,0:T(1,128)S(1)}, f32[16,1,1024]{2,1,0:T(1,128)S(1)}, u32[]{:S(2)}, u32[]{:S(2)}) collective-permute-start(f32[16,1,1024]{2,1,0:T(1,128)S(1)} %get-tuple-element.8), channel_id=1, source_target_pairs={{0,32},{32,64},{64,96},{96,128},{128,160},{160,192},{192,224},{1,3... | collective-permute-start | bytes 196616 | tf_op jit(solution)/shard_map/ppermute | solution.py:17
  56.3 13.4 %copy-start.1 = (bf16[16,512]{1,0:T(8,128)(2,1)S(1)}, bf16[16,512]{1,0:T(8,128)(2,1)}, u32[]{:S(2)}) copy-start(bf16[16,512]{1,0:T(8,128)(2,1)} %param.5) | copy-start | bytes 49156
  58.8 101.5 %all-to-all-start = ((bf16[16,32,2048]{2,0,1:T(8,128)(2,1)}), bf16[16,32,2048]{2,0,1:T(8,128)(2,1)S(1)}, u32[]{:S(2)}, u32[]{:S(2)}) async-start(bf16[16,32,2048]{2,0,1:T(8,128)(2,1)} %copy.8), calls=%async_computation | async-start | bytes 4194304 | tf_op jit(solution)/shard_map/all_to_all | solution.py:64
where the time goes:
time: 167 us
  blocking collectives  90.6 us (54%)
  starting transfers between devices  28.4 us (17%)
  other arithmetic  23.4 us (14%)
  waiting for transfers between devices  11.2 us (7%)
  local copies, waits for them, and re-layouts  10.5 us (6%)
  matrix products  2.65 us (2%)
    all_gather x1, blocking collectives, local(): lax.all_gather(rotation, 'st', axis=0, tiled=True)  90.6 us
    ppermute x4, waiting for transfers between devices, extended(): lax.ppermute(lax.slice_in_dim(block, block.shape[dim] - width, None, axis...  11.2 us
    all_to_all x1, starting transfers between devices, local(): lax.all_to_all(filtered, 'st', split_axis=1, concat_axis=0, tiled=True)  10.9 us
    sub x2, other arithmetic, chebyshev(): 2.0 * (apply_fn(current) - cheb_shift * current) / cheb_scale - previous  10.8 us
    ppermute x4, starting transfers between devices, extended(): lax.ppermute(lax.slice_in_dim(block, block.shape[dim] - width, None, axis...  9.57 us
    ppermute x4, starting transfers between devices, extended(): lax.ppermute(lax.slice_in_dim(block, 0, width, axis=dim), axis, backward)  7.92 us
    convert_element_type x1, other arithmetic, local(): result.astype(jnp.bfloat16).reshape(states_dev, planes * row_width)  5.77 us
    all_to_all x2, local copies, waits for them, and re-layouts, local(): lax.all_to_all(filtered, 'st', split_axis=1, concat_axis=0, tiled=True)  5.14 us
  transfers between devices with their start and end apart: 9, of which 4 were waited for; matrix products, arithmetic and copies ran while one was open for 1% of the time, Pallas kernels for 0%

commit v1 on v0

--- a/solution.py
+++ b/solution.py
@@ -2,6 +2,7 @@
 import jax.numpy as jnp
 from jax import lax
 from jax.sharding import PartitionSpec as P
+from jax.lax import all_to_all, axis_size
 
 DEGREE = 4
 NZ = 32
@@ -63,7 +64,7 @@
     filtered = result.astype(jnp.bfloat16).reshape(states_dev, planes * row_width)
     regrouped = lax.all_to_all(filtered, "st", split_axis=1, concat_axis=0, tiled=True)
     product = jnp.dot(
-        lax.all_gather(rotation, "st", axis=0, tiled=True),
+        jnp.concatenate(all_to_all(jnp.stack(axis_size("st") * [rotation]), "st", 0, 0), axis=0),
         regrouped,
         preferred_element_type=jnp.float32,
     )

time: 167 us -> 145 us (0.87)
  blocking collectives: 90.6 us -> 61.1 us
  other arithmetic: 23.4 us -> 33.5 us
  waiting for transfers between devices: 11.2 us -> 8.21 us
    all_gather x1 -> x0, blocking collectives: 90.6 us -> none  [local(): lax.all_gather(rotation, 'st', axis=0, tiled=True)]
    all_to_all x0 -> x1, blocking collectives: none -> 61.1 us  [local(): lax.all_to_all(filtered, 'st', split_axis=1, concat_axis=0, tiled=True)]
    convert_element_type x1, other arithmetic: 5.77 us -> 16 us  [local(): result.astype(jnp.bfloat16).reshape(states_dev, planes * row_width)]
    ppermute x4, waiting for transfers between devices: 11.2 us -> 8.2 us  [extended(): lax.ppermute(lax.slice_in_dim(block, block.shape[dim] - width, None, axis...]
    unnamed x4 -> x8, local copies, waits for them, and re-layouts: 0.01 us -> 1.88 us
  transfers between devices with their start and end apart: 9 -> 9, of which waited for: 4 -> 3; matrix products, arithmetic and copies ran while one was open for 1% -> 15% of each run, Pallas kernels for 0% -> 0%
where the time goes in v1:
time: 145 us; the launch traced here: 144 us
  blocking collectives  61.1 us (42%)
  other arithmetic  33.5 us (23%)
  starting transfers between devices  28.3 us (20%)
  local copies, waits for them, and re-layouts  11.5 us (8%)
  waiting for transfers between devices  8.21 us (6%)
    all_to_all x1, blocking collectives, local(): lax.all_to_all(filtered, 'st', split_axis=1, concat_axis=0, tiled=True)  61.1 us
    convert_element_type x1, other arithmetic, local(): result.astype(jnp.bfloat16).reshape(states_dev, planes * row_width)  16 us
    all_to_all x1, starting transfers between devices, local(): all_to_all(jnp.stack(axis_size('st') * [rotation]), 'st', 0, 0)  11.1 us
    sub x2, other arithmetic, chebyshev(): 2.0 * (apply_fn(current) - cheb_shift * current) / cheb_scale - previous  10.8 us
    ppermute x4, starting transfers between devices, extended(): lax.ppermute(lax.slice_in_dim(block, block.shape[dim] - width, None, axis...  9.39 us
    ppermute x4, waiting for transfers between devices, extended(): lax.ppermute(lax.slice_in_dim(block, block.shape[dim] - width, None, axis...  8.2 us
    ppermute x4, starting transfers between devices, extended(): lax.ppermute(lax.slice_in_dim(block, 0, width, axis=dim), axis, backward)  7.91 us
    all_to_all x2, local copies, waits for them, and re-layouts, local(): lax.all_to_all(filtered, 'st', split_axis=1, concat_axis=0, tiled=True)  4.88 us
  transfers between devices with their start and end apart: 9, of which 3 were waited for; matrix products, arithmetic and copies ran while one was open for 15% of the time, Pallas kernels for 0%

profile of v1, /device:TPU:2, one launch (start us, length us, event | category | flops | bytes accessed | tf_op | source)
XLA Modules:
  0.0 144.3 jit_solution(11297244312795342936)
XLA Ops:
  0.0 1.1 fusion.57
  1.2 1.9 %collective-permute-start = (f32[16,1,1024]{2,1,0:T(1,128)S(1)}, f32[16,1,1024]{2,1,0:T(1,128)S(1)}, u32[]{:S(2)}, u32[]{:S(2)}) collective-permute-start(f32[16,1,1024]{2,1,0:T(1,128)S(1)} %get-tuple-element.13), channel_id=1, source_target_pairs={{32,0},{64,32},{96,64},{128,96},{160,128},{192,160},{224,192},{33,... | collective-permute-start | bytes 196616 | tf_op jit(solution)/shard_map/ppermute | solution.py:21
  3.1 2.4 %collective-permute-start.1 = (f32[16,1,1024]{2,1,0:T(1,128)S(1)}, f32[16,1,1024]{2,1,0:T(1,128)S(1)}, u32[]{:S(2)}, u32[]{:S(2)}) collective-permute-start(f32[16,1,1024]{2,1,0:T(1,128)S(1)} %get-tuple-element.14), channel_id=1, source_target_pairs={{0,32},{32,64},{64,96},{96,128},{128,160},{160,192},{192,224},{1,3... | collective-permute-start | bytes 196616 | tf_op jit(solution)/shard_map/ppermute | solution.py:18
  5.5 2.0 %convert_element_type.21 = f32[16,64,1024]{2,1,0:T(8,128)S(1)} convert(bf16[16,64,1024]{2,1,0:T(8,128)(2,1)} %param.3) | non-fusion elementwise | flops 1048576 | bytes 6291456 | tf_op jit(solution)/shard_map/convert_element_type | solution.py:55
  7.6 1.6 %collective-permute-done.1 = f32[16,1,1024]{2,1,0:T(1,128)S(1)} collective-permute-done((f32[16,1,1024]{2,1,0:T(1,128)S(1)}, f32[16,1,1024]{2,1,0:T(1,128)S(1)}, u32[]{:S(2)}, u32[]{:S(2)}) %collective-permute-start.1) | collective-permute-done | bytes 65568 | tf_op jit(solution)/shard_map/ppermute | solution.py:18
  9.3 4.7 %broadcast_multiply_fusion = (f32[16,64,1024]{2,1,0:T(8,128)S(1)}, f32[16,64,1024]{2,1,0:T(8,128)S(1)}) fusion(f32[16,64,1024]{2,1,0:T(8,128)S(1)} %convert_element_type.21, pred[1024]{0:T(1024)(128)(4,1)S(1)} %get-tuple-element.17, pred[1024]{0:T(1024)(128)(4,1)S(1)} %get-tuple-element.18, f32[16,1,1024]{2,1,0:T(1,128)S(1)} %collective-permute-done.1, ...), kind=kLoop, calls=%fused_computation.73 | loop fusion | flops 15728640 | bytes 12978176 | tf_op jit(solution)/shard_map/div | solution.py:46
  14.0 2.2 %collective-permute-start.2 = (f32[16,1,1024]{2,1,0:T(1,128)S(1)}, f32[16,1,1024]{2,1,0:T(1,128)S(1)}, u32[]{:S(2)}, u32[]{:S(2)}) collective-permute-start(f32[16,1,1024]{2,1,0:T(1,128)S(1)} %get-tuple-element.11), channel_id=1, source_target_pairs={{32,0},{64,32},{96,64},{128,96},{160,128},{192,160},{224,192},{33,... | collective-permute-start | bytes 196616 | tf_op jit(solution)/shard_map/ppermute | solution.py:21
  16.2 2.2 %collective-permute-start.3 = (f32[16,1,1024]{2,1,0:T(1,128)S(1)}, f32[16,1,1024]{2,1,0:T(1,128)S(1)}, u32[]{:S(2)}, u32[]{:S(2)}) collective-permute-start(f32[16,1,1024]{2,1,0:T(1,128)S(1)} %get-tuple-element.12), channel_id=1, source_target_pairs={{0,32},{32,64},{64,96},{96,128},{128,160},{160,192},{192,224},{1,3... | collective-permute-start | bytes 196616 | tf_op jit(solution)/shard_map/ppermute | solution.py:18
  18.4 3.4 %collective-permute-done.3 = f32[16,1,1024]{2,1,0:T(1,128)S(1)} collective-permute-done((f32[16,1,1024]{2,1,0:T(1,128)S(1)}, f32[16,1,1024]{2,1,0:T(1,128)S(1)}, u32[]{:S(2)}, u32[]{:S(2)}) %collective-permute-start.3) | collective-permute-done | bytes 65568 | tf_op jit(solution)/shard_map/ppermute | solution.py:18
  21.8 6.1 %fusion.17 = f32[16,64,1024]{2,1,0:T(8,128)S(1)} fusion(f32[16,64,1024]{2,1,0:T(8,128)S(1)} %get-tuple-element.5, f32[16,1,1024]{2,1,0:T(1,128)S(1)} %collective-permute-done.3, f32[16,1,1024]{2,1,0:T(1,128)S(1)} %collective-permute-done.2, f32[16,64,1024]{2,1,0:T(8,128)S(1)} %get-tuple-element.6, f32[64,1024]{1,0:T(8,128)S(1)} %get-tuple-element.15, ...), kind=kLoop, calls=%fused_computation.33 | loop fusion | flops 17825792 | bytes 15075328 | tf_op jit(solution)/shard_map/sub | solution.py:48
  28.0 1.9 %collective-permute-start.4 = (f32[16,1,1024]{2,1,0:T(1,128)S(1)}, f32[16,1,1024]{2,1,0:T(1,128)S(1)}, u32[]{:S(2)}, u32[]{:S(2)}) collective-permute-start(f32[16,1,1024]{2,1,0:T(1,128)S(1)} %get-tuple-element.9), channel_id=1, source_target_pairs={{32,0},{64,32},{96,64},{128,96},{160,128},{192,160},{224,192},{33,... | collective-permute-start | bytes 196616 | tf_op jit(solution)/shard_map/ppermute | solution.py:21
  30.0 2.4 %collective-permute-start.5 = (f32[16,1,1024]{2,1,0:T(1,128)S(1)}, f32[16,1,1024]{2,1,0:T(1,128)S(1)}, u32[]{:S(2)}, u32[]{:S(2)}) collective-permute-start(f32[16,1,1024]{2,1,0:T(1,128)S(1)} %get-tuple-element.10), channel_id=1, source_target_pairs={{0,32},{32,64},{64,96},{96,128},{128,160},{160,192},{192,224},{1,3... | collective-permute-start | bytes 196616 | tf_op jit(solution)/shard_map/ppermute | solution.py:18
  32.4 3.2 %collective-permute-done.5 = f32[16,1,1024]{2,1,0:T(1,128)S(1)} collective-permute-done((f32[16,1,1024]{2,1,0:T(1,128)S(1)}, f32[16,1,1024]{2,1,0:T(1,128)S(1)}, u32[]{:S(2)}, u32[]{:S(2)}) %collective-permute-start.5) | collective-permute-done | bytes 65568 | tf_op jit(solution)/shard_map/ppermute | solution.py:18
  35.6 4.7 %fusion.28 = f32[16,64,1024]{2,1,0:T(8,128)S(1)} fusion(f32[16,64,1024]{2,1,0:T(8,128)S(1)} %fusion.17, f32[16,1,1024]{2,1,0:T(1,128)S(1)} %collective-permute-done.5, f32[16,1,1024]{2,1,0:T(1,128)S(1)} %collective-permute-done.4, f32[16,64,1024]{2,1,0:T(8,128)S(1)} %get-tuple-element.6, f32[64,1024]{1,0:T(8,128)S(1)} %get-tuple-element.16, ...), kind=kLoop, calls=%fused_computation.44 | loop fusion | flops 17825792 | bytes 12978176 | tf_op jit(solution)/shard_map/sub | solution.py:48
  40.4 1.9 %copy-done.1 = f32[16,64,1024]{2,1,0:T(8,128)} copy-done((f32[16,64,1024]{2,1,0:T(8,128)}, f32[16,64,1024]{2,1,0:T(8,128)S(1)}, u32[]{:S(2)}) %copy-start.1) | copy-done | bytes 4194328
  42.3 1.9 %collective-permute-start.6 = (f32[16,1,1024]{2,1,0:T(1,128)S(1)}, f32[16,1,1024]{2,1,0:T(1,128)S(1)}, u32[]{:S(2)}, u32[]{:S(2)}) collective-permute-start(f32[16,1,1024]{2,1,0:T(1,128)S(1)} %get-tuple-element.7), channel_id=1, source_target_pairs={{32,0},{64,32},{96,64},{128,96},{160,128},{192,160},{224,192},{33,... | collective-permute-start | bytes 196616 | tf_op jit(solution)/shard_map/ppermute | solution.py:21
  44.2 2.4 %collective-permute-start.7 = (f32[16,1,1024]{2,1,0:T(1,128)S(1)}, f32[16,1,1024]{2,1,0:T(1,128)S(1)}, u32[]{:S(2)}, u32[]{:S(2)}) collective-permute-start(f32[16,1,1024]{2,1,0:T(1,128)S(1)} %get-tuple-element.8), channel_id=1, source_target_pairs={{0,32},{32,64},{64,96},{96,128},{128,160},{160,192},{192,224},{1,3... | collective-permute-start | bytes 196616 | tf_op jit(solution)/shard_map/ppermute | solution.py:18
  47.5 11.1 %all-to-all-start.1 = ((bf16[32,16,512]{2,1,0:T(8,128)(2,1)}), bf16[32,16,512]{2,1,0:T(8,128)(2,1)S(1)}, u32[]{:S(2)}, u32[]{:S(2)}) async-start(bf16[32,16,512]{2,1,0:T(8,128)(2,1)} %stack.2), calls=%async_computation.1 | async-start | bytes 1048576 | tf_op jit(solution)/shard_map/all_to_all | solution.py:67
  58.6 16.0 %fusion.40 = bf16[16,64,1024]{2,1,0:T(8,128)(2,1)S(1)} fusion(f32[16,64,1024]{2,1,0:T(8,128)} %copy-done, f32[16,64,1024]{2,1,0:T(8,128)} %copy-done.1, f32[16,1,1024]{2,1,0:T(1,128)S(1)} %collective-permute-done.7, f32[16,1,1024]{2,1,0:T(1,128)S(1)} %collective-permute-done.6, f32[64,1024]{1,0:T(8,128)S(1)} %get-tuple-element.16, ...), kind=kLoop, calls=%fused_computation.56 | loop fusion | flops 17825792 | bytes 10881024 | tf_op jit(solution)/shard_map/convert_element_type | solution.py:64
  74.6 2.1 %all_to_all.17 = bf16[16,32,2048]{2,1,0:T(8,128)(2,1)} reshape(bf16[16,64,1024]{2,1,0:T(8,128)(2,1)S(1)} %fusion.40) | data formatting | bytes 4194304 | tf_op jit(solution)/shard_map/all_to_all | solution.py:65
  76.7 2.7 %copy.8 = bf16[16,32,2048]{2,0,1:T(8,128)(2,1)S(1)} copy(bf16[16,32,2048]{2,1,0:T(8,128)(2,1)} %all_to_all.17) | data formatting | bytes 4194304 | tf_op jit(solution)/shard_map/all_to_all | solution.py:65
  79.5 61.1 %all_to_all.24 = bf16[16,32,2048]{2,0,1:T(8,128)(2,1)S(1)} all-to-all(bf16[16,32,2048]{2,0,1:T(8,128)(2,1)S(1)} %copy.8), channel_id=1, replica_groups=mesh['dom'=8,'st'=32] {'st'}, dimensions={1} | all-to-all | bytes 4194304 | tf_op jit(solution)/shard_map/all_to_all | solution.py:65
  140.6 1.3 fusion.47
  141.9 2.4 %copy.9 = bf16[512,2048]{1,0:T(8,128)(2,1)} copy(bf16[512,2048]{0,1:T(8,128)(2,1)S(1)} %fusion.47) | data formatting | bytes 4194304 | tf_op jit(solution)/shard_map/convert_element_type | solution.py:71
  (19 shorter events, 1.3 us)
Async XLA Ops:
  0.0 7.6 %copy-start.2 = (bf16[64,1024]{1,0:T(8,128)(2,1)S(1)}, bf16[64,1024]{1,0:T(8,128)(2,1)}, u32[]{:S(2)}) copy-start(bf16[64,1024]{1,0:T(8,128)(2,1)} %param.4) | copy-start | bytes 393220
  1.2 6.5 %collective-permute-start = (f32[16,1,1024]{2,1,0:T(1,128)S(1)}, f32[16,1,1024]{2,1,0:T(1,128)S(1)}, u32[]{:S(2)}, u32[]{:S(2)}) collective-permute-start(f32[16,1,1024]{2,1,0:T(1,128)S(1)} %get-tuple-element.13), channel_id=1, source_target_pairs={{32,0},{64,32},{96,64},{128,96},{160,128},{192,160},{224,192},{33,... | collective-permute-start | bytes 196616 | tf_op jit(solution)/shard_map/ppermute | solution.py:21
  3.1 6.2 %collective-permute-start.1 = (f32[16,1,1024]{2,1,0:T(1,128)S(1)}, f32[16,1,1024]{2,1,0:T(1,128)S(1)}, u32[]{:S(2)}, u32[]{:S(2)}) collective-permute-start(f32[16,1,1024]{2,1,0:T(1,128)S(1)} %get-tuple-element.14), channel_id=1, source_target_pairs={{0,32},{32,64},{64,96},{96,128},{128,160},{160,192},{192,224},{1,3... | collective-permute-start | bytes 196616 | tf_op jit(solution)/shard_map/ppermute | solution.py:18
  14.0 4.3 %collective-permute-start.2 = (f32[16,1,1024]{2,1,0:T(1,128)S(1)}, f32[16,1,1024]{2,1,0:T(1,128)S(1)}, u32[]{:S(2)}, u32[]{:S(2)}) collective-permute-start(f32[16,1,1024]{2,1,0:T(1,128)S(1)} %get-tuple-element.11), channel_id=1, source_target_pairs={{32,0},{64,32},{96,64},{128,96},{160,128},{192,160},{224,192},{33,... | collective-permute-start | bytes 196616 | tf_op jit(solution)/shard_map/ppermute | solution.py:21
  16.2 5.6 %collective-permute-start.3 = (f32[16,1,1024]{2,1,0:T(1,128)S(1)}, f32[16,1,1024]{2,1,0:T(1,128)S(1)}, u32[]{:S(2)}, u32[]{:S(2)}) collective-permute-start(f32[16,1,1024]{2,1,0:T(1,128)S(1)} %get-tuple-element.12), channel_id=1, source_target_pairs={{0,32},{32,64},{64,96},{96,128},{128,160},{160,192},{192,224},{1,3... | collective-permute-start | bytes 196616 | tf_op jit(solution)/shard_map/ppermute | solution.py:18
  27.9 12.4 %copy-start = (f32[16,64,1024]{2,1,0:T(8,128)}, f32[16,64,1024]{2,1,0:T(8,128)S(1)}, u32[]{:S(2)}) copy-start(f32[16,64,1024]{2,1,0:T(8,128)S(1)} %fusion.17) | copy-start | bytes 12582916
  28.0 4.4 %collective-permute-start.4 = (f32[16,1,1024]{2,1,0:T(1,128)S(1)}, f32[16,1,1024]{2,1,0:T(1,128)S(1)}, u32[]{:S(2)}, u32[]{:S(2)}) collective-permute-start(f32[16,1,1024]{2,1,0:T(1,128)S(1)} %get-tuple-element.9), channel_id=1, source_target_pairs={{32,0},{64,32},{96,64},{128,96},{160,128},{192,160},{224,192},{33,... | collective-permute-start | bytes 196616 | tf_op jit(solution)/shard_map/ppermute | solution.py:21
  30.0 16.6 %copy-start.3 = (bf16[16,512]{1,0:T(8,128)(2,1)S(1)}, bf16[16,512]{1,0:T(8,128)(2,1)}, u32[]{:S(2)}) copy-start(bf16[16,512]{1,0:T(8,128)(2,1)} %param.5) | copy-start | bytes 49156
  30.0 5.6 %collective-permute-start.5 = (f32[16,1,1024]{2,1,0:T(1,128)S(1)}, f32[16,1,1024]{2,1,0:T(1,128)S(1)}, u32[]{:S(2)}, u32[]{:S(2)}) collective-permute-start(f32[16,1,1024]{2,1,0:T(1,128)S(1)} %get-tuple-element.10), channel_id=1, source_target_pairs={{0,32},{32,64},{64,96},{96,128},{128,160},{160,192},{192,224},{1,3... | collective-permute-start | bytes 196616 | tf_op jit(solution)/shard_map/ppermute | solution.py:18
  40.3 2.0 %copy-start.1 = (f32[16,64,1024]{2,1,0:T(8,128)}, f32[16,64,1024]{2,1,0:T(8,128)S(1)}, u32[]{:S(2)}) copy-start(f32[16,64,1024]{2,1,0:T(8,128)S(1)} %fusion.28) | copy-start | bytes 12582916
  42.3 16.3 %collective-permute-start.6 = (f32[16,1,1024]{2,1,0:T(1,128)S(1)}, f32[16,1,1024]{2,1,0:T(1,128)S(1)}, u32[]{:S(2)}, u32[]{:S(2)}) collective-permute-start(f32[16,1,1024]{2,1,0:T(1,128)S(1)} %get-tuple-element.7), channel_id=1, source_target_pairs={{32,0},{64,32},{96,64},{128,96},{160,128},{192,160},{224,192},{33,... | collective-permute-start | bytes 196616 | tf_op jit(solution)/shard_map/ppermute | solution.py:21
  44.2 14.4 %collective-permute-start.7 = (f32[16,1,1024]{2,1,0:T(1,128)S(1)}, f32[16,1,1024]{2,1,0:T(1,128)S(1)}, u32[]{:S(2)}, u32[]{:S(2)}) collective-permute-start(f32[16,1,1024]{2,1,0:T(1,128)S(1)} %get-tuple-element.8), channel_id=1, source_target_pairs={{0,32},{32,64},{64,96},{96,128},{128,160},{160,192},{192,224},{1,3... | collective-permute-start | bytes 196616 | tf_op jit(solution)/shard_map/ppermute | solution.py:18
  47.5 32.0 %all-to-all-start.1 = ((bf16[32,16,512]{2,1,0:T(8,128)(2,1)}), bf16[32,16,512]{2,1,0:T(8,128)(2,1)S(1)}, u32[]{:S(2)}, u32[]{:S(2)}) async-start(bf16[32,16,512]{2,1,0:T(8,128)(2,1)} %stack.2), calls=%async_computation.1 | async-start | bytes 1048576 | tf_op jit(solution)/shard_map/all_to_all | solution.py:67
